TPU v7x, 32 devices: a whole 2x2x4 slice. The times are simulated.
32 devices in a mesh: gx: 8 (over y, x, core), gy: 4 (over z).
Axes of the slice: x: 2, y: 2, z: 4, core: 2. Of those that a mesh axis runs over, the one named last changes fastest.
Arguments:
- species_field: float32 [168, 156, 672], P('gx', 'gy'), as said below
- start_block: float32 [672, 128], replicated, may hold values from -6 to 6
- trunc_ranks: int32 [3], replicated, may hold values from 64 to 128, as said below
Outputs:
- core_field: float32 [128, 156, 168], P('gx', 'gy')
- energies: float32 [128], replicated
Inputs may be any that keep to these rules, and one draw needn't show every extreme that they name: `trunc_ranks`: entry 0 is the rank used in this mode step; one of the three entries equals 128. `species_field`: finite values.
All inputs are finite; a program needn't handle non-finite values.
Results may differ from a plain program's by a relative error of at most 0.00045.
Values sent between devices are 32-bit elements; how exact they have to be, the bound alone decides.
No kernel may reach another device: no remote copies, remote signals or barrier semaphores. Data moves between devices by JAX's collectives and lax.ppermute only.
A program may use at most 64 MiB of HBM per device.

v0:
```python
import functools

import jax
import jax.numpy as jnp
from jax import lax
from jax.experimental import pallas as pl
from jax.experimental.pallas import tpu as pltpu
from jax.sharding import PartitionSpec as P

ITERS = 3
LANES = 128
HIGHEST = lax.Precision.HIGHEST
F32 = jnp.float32
BF16 = jnp.bfloat16


def split(value):
    high = value.astype(BF16)
    return high, (value - high.astype(F32)).astype(BF16)


def dot(left, right, left_dim=1, right_dim=0, precision=None):
    return lax.dot_general(
        left,
        right,
        (((left_dim,), (right_dim,)), ((), ())),
        precision=precision,
        preferred_element_type=F32,
    )


def packed_blocks(order):
    full, rest = divmod(order, LANES)
    blocks, row = {}, 0
    for i in range(full):
        for j in range(i, full):
            blocks[i, j] = row
            row += LANES
    if rest:
        for j in range(full + 1):
            blocks[full, j] = row
            row += rest
    return blocks, row


def gram_kernel(x_ref, out_ref, flat, high, low):
    slabs, rows, order = x_ref.shape
    pitch = -(-rows // 8) * 8
    for b in range(slabs):
        flat[pl.ds(b * pitch, rows), :] = x_ref[b]
        if pitch > rows:
            flat[pl.ds(b * pitch + rows, pitch - rows), :] = jnp.zeros((pitch - rows, order), F32)
    spare = flat.shape[0] - slabs * pitch
    if spare:
        flat[pl.ds(slabs * pitch, spare), :] = jnp.zeros((spare, order), F32)
    h, l = split(flat[...])
    high[...] = h
    low[...] = l
    full, rest = divmod(order, LANES)
    blocks, _ = packed_blocks(order)
    for i in range(full):
        rows_i = slice(i * LANES, (i + 1) * LANES)
        cols = slice(i * LANES, full * LANES)
        product = (
            dot(high[:, rows_i], high[:, cols], 0, 0)
            + dot(high[:, rows_i], low[:, cols], 0, 0)
            + dot(low[:, rows_i], high[:, cols], 0, 0)
        )
        for j in range(i, full):
            out_ref[pl.ds(blocks[i, j], LANES), :] = product[:, (j - i) * LANES : (j - i + 1) * LANES]
    if rest:
        rows_i = slice(full * LANES, order)
        product = (
            dot(high[:, rows_i], high[...], 0, 0)
            + dot(high[:, rows_i], low[...], 0, 0)
            + dot(low[:, rows_i], high[...], 0, 0)
        )
        for j in range(full):
            out_ref[pl.ds(blocks[full, j], rest), :] = product[:, j * LANES : (j + 1) * LANES]
        corner = product[:, full * LANES :]
        out_ref[pl.ds(blocks[full, full], rest), :] = jnp.concatenate(
            [corner, jnp.zeros((rest, LANES - rest), F32)], axis=1
        )


def gram_blocks(x):
    slabs, rows, order = x.shape
    depth = -(-slabs * (-(-rows // 8) * 8) // 16) * 16
    _, packed = packed_blocks(order)
    return pl.pallas_call(
        gram_kernel,
        out_shape=jax.ShapeDtypeStruct((packed, LANES), F32),
        scratch_shapes=[
            pltpu.VMEM((depth, order), F32),
            pltpu.VMEM((depth, order), BF16),
            pltpu.VMEM((depth, order), BF16),
        ],
        compiler_params=pltpu.CompilerParams(vmem_limit_bytes=32 << 20),
        name="gram",
    )(x)


def all_sum(value, sizes):
    count_x, count_y = sizes
    ix, iy = lax.axis_index("gx"), lax.axis_index("gy")
    colour = ix & 1
    bits_x = [1 << b for b in range(count_x.bit_length() - 1)]
    bits_y = [1 << b for b in range(count_y.bit_length() - 1)]
    stages_x = list(zip(bits_x[:1], bits_x[:1])) + list(zip(bits_x[1:], reversed(bits_x[1:])))
    stages_y = list(zip(bits_y, reversed(bits_y)))

    def swap(data, flip_x, flip_y):
        pairs = []
        for i in range(count_x):
            for j in range(count_y):
                other = (i ^ flip_x[i & 1]) * count_y + (j ^ flip_y[i & 1])
                pairs.append((i * count_y + j, other))
        return lax.ppermute(data, ("gx", "gy"), pairs)

    for flip in stages_x:
        half = value.shape[0] // 2
        upper = (ix & jnp.where(colour == 0, flip[0], flip[1])) != 0
        keep = jnp.where(upper, half, 0)
        send = lax.dynamic_slice(value, (half - keep, 0), (half, value.shape[1]))
        kept = lax.dynamic_slice(value, (keep, 0), (half, value.shape[1]))
        value = kept + swap(send, flip, (0, 0))
    for flip in stages_y:
        value = value + swap(value, (0, 0), flip)
    for flip in reversed(stages_x):
        upper = (ix & jnp.where(colour == 0, flip[0], flip[1])) != 0
        other = swap(value, flip, (0, 0))
        value = jnp.concatenate([jnp.where(upper, other, value), jnp.where(upper, value, other)], axis=0)
    return value


def eliminate(scaled):
    size = scaled.shape[0]
    lane = lax.broadcasted_iota(jnp.int32, (1, size), 1)
    sub = lax.broadcasted_iota(jnp.int32, (8, 1), 0)
    blocks = [scaled[8 * i : 8 * i + 8, :] for i in range(size // 8)]
    for j in range(size):
        own, at = divmod(j, 8)
        row = blocks[own][at : at + 1, :]
        pivot = (row + jnp.where(lane == j, 1.0, 0.0)) * (1.0 / row[:, j : j + 1])
        for b in range(own, size // 8):
            column = blocks[b][:, j : j + 1]
            if b == own:
                if at == 7:
                    continue
                column = jnp.where(sub > at, column, 0.0)
            blocks[b] = blocks[b] - column * pivot
    return jnp.concatenate(blocks, axis=0)


def orthonormal(columns):
    size = columns.shape[1]
    i = lax.broadcasted_iota(jnp.int32, (size, size), 0)
    j = lax.broadcasted_iota(jnp.int32, (size, size), 1)
    cross_gram = dot(columns, columns, 0, 0, HIGHEST)
    diagonal = jnp.where(i == j, cross_gram, 0.0)
    scale_row = lax.rsqrt(jnp.sum(diagonal, axis=0, keepdims=True))
    scale_col = lax.rsqrt(jnp.sum(diagonal, axis=1, keepdims=True))
    done = eliminate(cross_gram * scale_row * scale_col)
    pivots = jnp.sum(jnp.where(i == j, done, 0.0), axis=1, keepdims=True)
    unit = jnp.where(i > j, done, jnp.where(i == j, 1.0, 0.0))
    inverse = unit * lax.rsqrt(pivots) * scale_row
    return dot(columns, inverse, 1, 1, HIGHEST)


def subspace_kernel(ranks_ref, packed_ref, start_ref, xh_ref, xl_ref, core_ref, energy_ref, gram_high, gram_low, basis):
    order, size = start_ref.shape
    blocks, _ = packed_blocks(order)
    full, rest = divmod(order, LANES)

    trace = jnp.zeros((1, 1), F32)
    for (i, j), row in blocks.items():
        height = LANES if i < full else rest
        width = LANES if j < full else rest
        block = packed_ref[pl.ds(row, height), :][:, :width]
        if i == j:
            a = lax.broadcasted_iota(jnp.int32, (height, width), 0)
            b = lax.broadcasted_iota(jnp.int32, (height, width), 1)
            trace = trace + jnp.sum(jnp.where(a == b, block, 0.0), keepdims=True)
        h, l = split(block)
        gram_high[i * LANES : i * LANES + height, j * LANES : j * LANES + width] = h
        gram_low[i * LANES : i * LANES + height, j * LANES : j * LANES + width] = l
        if i != j:
            h, l = split(block.T)
            gram_high[j * LANES : j * LANES + width, i * LANES : i * LANES + height] = h
            gram_low[j * LANES : j * LANES + width, i * LANES : i * LANES + height] = l

    def images(subspace):
        h, l = split(subspace)
        both = dot(gram_high[...], jnp.concatenate([h, l], axis=1))
        return both[:, :size] + both[:, size:] + dot(gram_low[...], h)

    basis[...] = start_ref[...]

    def step(_, carry):
        basis[...] = orthonormal(images(basis[...]))
        return carry

    lax.fori_loop(0, ITERS, step, 0)
    lane = lax.broadcasted_iota(jnp.int32, (1, size), 1)
    masked = basis[...] * jnp.where(lane < ranks_ref[0], 1.0, 0.0)
    h, l = split(masked)
    core = dot(h, xh_ref[...], 0, 0) + dot(h, xl_ref[...], 0, 0) + dot(l, xh_ref[...], 0, 0)
    parts, rows, _ = core_ref.shape
    for p in range(parts):
        core_ref[p] = core[p * rows : (p + 1) * rows, :]
    caught = jnp.sum(masked * images(masked), axis=0, keepdims=True)
    energy_ref[...] = caught / (trace / order)


def subspace_step(ranks, packed, start, x_high, x_low, parts):
    order, size = start.shape
    vmem = pl.BlockSpec(memory_space=pltpu.VMEM)
    return pl.pallas_call(
        subspace_kernel,
        in_specs=[pl.BlockSpec(memory_space=pltpu.SMEM)] + [vmem] * 4,
        out_specs=[vmem, vmem],
        out_shape=(
            jax.ShapeDtypeStruct((parts, size // parts, x_high.shape[1]), F32),
            jax.ShapeDtypeStruct((1, size), F32),
        ),
        scratch_shapes=[
            pltpu.VMEM((order, order), BF16),
            pltpu.VMEM((order, order), BF16),
            pltpu.VMEM((order, size), F32),
        ],
        compiler_params=pltpu.CompilerParams(vmem_limit_bytes=32 << 20),
        name="subspace",
    )(ranks, packed, start, x_high, x_low)


def arrange_kernel(slabs, blocks_ref, out_ref):
    for c in range(out_ref.shape[0]):
        pieces = [blocks_ref[s, :, c * slabs : (c + 1) * slabs] for s in range(blocks_ref.shape[0])]
        out_ref[c] = jnp.concatenate(pieces, axis=1)


def arrange(blocks, slabs, rows):
    parts, kept, _ = blocks.shape
    return pl.pallas_call(
        functools.partial(arrange_kernel, slabs),
        out_shape=jax.ShapeDtypeStruct((rows, kept, parts * slabs), F32),
        compiler_params=pltpu.CompilerParams(vmem_limit_bytes=32 << 20),
        name="arrange",
    )(blocks)


def shards(sizes, species_field, start_block, trunc_ranks):
    slabs, rows, order = species_field.shape
    packed = all_sum(gram_blocks(species_field), sizes)
    width = slabs * rows
    x_t = jnp.transpose(species_field, (2, 1, 0)).reshape(order, width)
    x_t = jnp.pad(x_t, ((0, 0), (0, -width % LANES)))
    rounded = lax.reduce_precision(x_t, 8, 7)
    x_high = rounded.astype(BF16)
    x_low = (x_t - rounded).astype(BF16)
    core, energies = subspace_step(trunc_ranks, packed, start_block, x_high, x_low, sizes[0])
    core = lax.all_to_all(core, "gx", split_axis=0, concat_axis=0, tiled=True)
    core = arrange(core, slabs, rows)
    return (jnp.transpose(core, (1, 0, 2)), energies[0])


def solution(mesh):
    sizes = (mesh.shape["gx"], mesh.shape["gy"])
    in_specs = (P("gx", "gy", None), P(), P())
    out_specs = (P("gx", "gy", None), P())
    return jax.shard_map(
        functools.partial(shards, sizes), mesh=mesh, in_specs=in_specs, out_specs=out_specs, check_vma=False
    )
```

profile of v0, /device:TPU:0, one launch (start us, length us, event | category | flops | bytes accessed | tf_op | source)
XLA Modules:
  0.0 110.5 jit_solution(16198651189130889421)
XLA Ops:
  0.6 0.0 copy-start
  0.6 1.7 %copy-done = f32[21,39,672]{2,1,0:T(8,128)S(1)} copy-done((f32[21,39,672]{2,1,0:T(8,128)S(1)}, f32[21,39,672]{2,1,0:T(8,128)}, u32[]{:S(2)}) %copy-start) | copy-done | bytes 2201496
  2.4 2.8 %gram.1 = f32[2112,128]{1,0:T(8,128)S(1)} custom-call(f32[21,39,672]{2,1,0:T(8,128)S(1)} %copy-done), custom_call_target="tpu_custom_call" | custom-call | tf_op jit(solution)/shard_map/gram/pallas_call | solution.py:90
  5.2 0.5 collective-permute-start
  5.7 1.6 %collective-permute-done = f32[1056,128]{1,0:T(8,128)S(1)} collective-permute-done((f32[1056,128]{1,0:T(8,128)S(1)}, f32[1056,128]{1,0:T(8,128)S(1)}, u32[]{:S(2)}, u32[]{:S(2)}) %collective-permute-start) | collective-permute-done | bytes 540704 | tf_op jit(solution)/shard_map/ppermute | solution.py:118
  7.3 0.1 dynamic-slice_add_fusion
  7.4 2.9 %collective-permute-start.1 = (f32[528,128]{1,0:T(8,128)S(1)}, f32[528,128]{1,0:T(8,128)S(1)}, u32[]{:S(2)}, u32[]{:S(2)}) collective-permute-start(f32[528,128]{1,0:T(8,128)S(1)} %constant_dynamic-slice_fusion.1), channel_id=1, source_target_pairs={{0,8},{1,9},{2,10},{3,11},{4,20},{5,21},{6,22},{7,23},{8,0},{9,1},... | collective-permute-start | bytes 811016 | tf_op jit(solution)/shard_map/ppermute | solution.py:118
  10.3 4.4 %collective-permute-done.1 = f32[528,128]{1,0:T(8,128)S(1)} collective-permute-done((f32[528,128]{1,0:T(8,128)S(1)}, f32[528,128]{1,0:T(8,128)S(1)}, u32[]{:S(2)}, u32[]{:S(2)}) %collective-permute-start.1) | collective-permute-done | bytes 270368 | tf_op jit(solution)/shard_map/ppermute | solution.py:118
  14.8 2.1 %collective-permute-start.2 = (f32[264,128]{1,0:T(8,128)S(1)}, f32[264,128]{1,0:T(8,128)S(1)}, u32[]{:S(2)}, u32[]{:S(2)}) collective-permute-start(f32[264,128]{1,0:T(8,128)S(1)} %constant_dynamic-slice_fusion), channel_id=1, source_target_pairs={{0,16},{1,17},{2,18},{3,19},{4,12},{5,13},{6,14},{7,15},{8,24},{9,... | collective-permute-start | bytes 405512 | tf_op jit(solution)/shard_map/ppermute | solution.py:118
  16.9 3.0 %collective-permute-done.2 = f32[264,128]{1,0:T(8,128)S(1)} collective-permute-done((f32[264,128]{1,0:T(8,128)S(1)}, f32[264,128]{1,0:T(8,128)S(1)}, u32[]{:S(2)}, u32[]{:S(2)}) %collective-permute-start.2) | collective-permute-done | bytes 135200 | tf_op jit(solution)/shard_map/ppermute | solution.py:118
  19.9 2.1 %collective-permute-start.3 = (f32[264,128]{1,0:T(8,128)S(1)}, f32[264,128]{1,0:T(8,128)S(1)}, u32[]{:S(2)}, u32[]{:S(2)}) collective-permute-start(f32[264,128]{1,0:T(8,128)S(1)} %dynamic-slice_add_fusion.2), channel_id=1, source_target_pairs={{0,1},{1,0},{2,3},{3,2},{4,6},{5,7},{6,4},{7,5},{8,9},{9,8},{10,11... | collective-permute-start | bytes 405512 | tf_op jit(solution)/shard_map/ppermute | solution.py:118
  22.1 3.4 %collective-permute-done.3 = f32[264,128]{1,0:T(8,128)S(1)} collective-permute-done((f32[264,128]{1,0:T(8,128)S(1)}, f32[264,128]{1,0:T(8,128)S(1)}, u32[]{:S(2)}, u32[]{:S(2)}) %collective-permute-start.3) | collective-permute-done | bytes 135200 | tf_op jit(solution)/shard_map/ppermute | solution.py:118
  25.5 2.7 %collective-permute-start.4 = (f32[264,128]{1,0:T(8,128)S(1)}, f32[264,128]{1,0:T(8,128)S(1)}, u32[]{:S(2)}, u32[]{:S(2)}) collective-permute-start(f32[264,128]{1,0:T(8,128)S(1)} %add.38), channel_id=1, source_target_pairs={{0,2},{1,3},{2,0},{3,1},{4,5},{5,4},{6,7},{7,6},{8,10},{9,11},{10,... | collective-permute-start | bytes 405512 | tf_op jit(solution)/shard_map/ppermute | solution.py:118
  28.2 3.3 %collective-permute-done.4 = f32[264,128]{1,0:T(8,128)S(1)} collective-permute-done((f32[264,128]{1,0:T(8,128)S(1)}, f32[264,128]{1,0:T(8,128)S(1)}, u32[]{:S(2)}, u32[]{:S(2)}) %collective-permute-start.4) | collective-permute-done | bytes 135200 | tf_op jit(solution)/shard_map/ppermute | solution.py:118
  31.5 3.4 %collective-permute-start.5 = (f32[264,128]{1,0:T(8,128)S(1)}, f32[264,128]{1,0:T(8,128)S(1)}, u32[]{:S(2)}, u32[]{:S(2)}) collective-permute-start(f32[264,128]{1,0:T(8,128)S(1)} %add.39), channel_id=1, source_target_pairs={{0,16},{1,17},{2,18},{3,19},{4,12},{5,13},{6,14},{7,15},{8,24},{9,... | collective-permute-start | bytes 405512 | tf_op jit(solution)/shard_map/ppermute | solution.py:118
  34.9 4.4 %collective-permute-done.5 = f32[264,128]{1,0:T(8,128)S(1)} collective-permute-done((f32[264,128]{1,0:T(8,128)S(1)}, f32[264,128]{1,0:T(8,128)S(1)}, u32[]{:S(2)}, u32[]{:S(2)}) %collective-permute-start.5) | collective-permute-done | bytes 135200 | tf_op jit(solution)/shard_map/ppermute | solution.py:118
  39.3 0.0 copy-start.1
  39.4 2.1 %collective-permute-start.6 = (f32[528,128]{1,0:T(8,128)S(1)}, f32[528,128]{1,0:T(8,128)S(1)}, u32[]{:S(2)}, u32[]{:S(2)}) collective-permute-start(f32[528,128]{1,0:T(8,128)S(1)} %pad_maximum_fusion.2), channel_id=1, source_target_pairs={{0,8},{1,9},{2,10},{3,11},{4,20},{5,21},{6,22},{7,23},{8,0},{9,1},... | collective-permute-start | bytes 811016 | tf_op jit(solution)/shard_map/ppermute | solution.py:118
  41.5 4.4 %collective-permute-done.6 = f32[528,128]{1,0:T(8,128)S(1)} collective-permute-done((f32[528,128]{1,0:T(8,128)S(1)}, f32[528,128]{1,0:T(8,128)S(1)}, u32[]{:S(2)}, u32[]{:S(2)}) %collective-permute-start.6) | collective-permute-done | bytes 270368 | tf_op jit(solution)/shard_map/ppermute | solution.py:118
  45.9 0.8 pad_maximum_fusion.1
  46.8 0.8 copy.6
  47.6 1.8 %reshape.7 = f32[672,819]{0,1:T(8,128)} reshape(f32[672,39,21]{0,2,1:T(8,128)S(1)} %copy.6) | data formatting | bytes 4402944 | tf_op jit(solution)/shard_map/reshape | solution.py:256
  49.4 2.4 %copy.7 = f32[672,819]{1,0:T(8,128)S(1)} copy(f32[672,819]{0,1:T(8,128)} %reshape.7) | data formatting | bytes 4402944 | tf_op jit(solution)/shard_map/reshape | solution.py:256
  51.8 0.3 fusion
  52.2 1.1 %broadcast_select_fusion.1 = (f32[1056,128]{1,0:T(8,128)S(1)}, f32[1056,128]{1,0:T(8,128)S(1)}) fusion(f32[1056,128]{1,0:T(8,128)} %collective-permute-done.7, pred[]{:T(512)S(6)} %ne.12, f32[528,128]{1,0:T(8,128)S(1)} %get-tuple-element.11, f32[528,128]{1,0:T(8,128)S(1)} %get-tuple-element.10), kind=kLoop, calls=%fused_computation.9 | loop fusion | flops 405504 | bytes 2162689 | tf_op jit(solution)/shard_map/jit(_where)/select_n | solution.py:132
  53.3 0.0 copy-start.2
  53.3 0.0 copy-start.3
  53.3 0.1 pad_maximum_fusion.packed_ref
  53.4 0.9 copy-done.2
  54.3 41.4 %subspace.1 = (f32[8,16,896]{2,1,0:T(8,128)S(1)}, f32[1,128]{1,0:T(1,128)}) custom-call(s32[3]{0:T(128)S(1)} %copy-done.3, f32[2112,128]{1,0:T(8,128)S(1)} %pad_maximum_fusion.packed_ref, f32[672,128]{1,0:T(8,128)S(1)} %copy-done.2, bf16[672,896]{1,0:T(8,128)(2,1)S(1)} %get-tuple-element.7.xh_ref, bf16[672,896]{1,0:T(8,128)(2,1)S(1)} %get-tuple-element.6.xl_ref), custom_call_target="tpu_custom_call" | custom-call | tf_op jit(solution)/shard_map/subspace/pallas_call | solution.py:218
  95.7 13.2 %all_to_all.5.blocks_ref = f32[8,16,896]{2,1,0:T(8,128)S(1)} all-to-all(f32[8,16,896]{2,1,0:T(8,128)S(1)} %get-tuple-element.4), channel_id=1, replica_groups=mesh['gx'=8,'gy'=4] {'gx'}, dimensions={0} | all-to-all | bytes 917504 | tf_op jit(solution)/shard_map/all_to_all | solution.py:262
  108.9 1.6 %arrange.1 = f32[39,16,168]{2,1,0:T(8,128)} custom-call(f32[8,16,896]{2,1,0:T(8,128)S(1)} %all_to_all.5.blocks_ref), custom_call_target="tpu_custom_call" | custom-call | tf_op jit(solution)/shard_map/arrange/pallas_call | solution.py:244
  (14 shorter events, 0.3 us)
Async XLA Ops:
  0.6 1.7 %copy-start = (f32[21,39,672]{2,1,0:T(8,128)S(1)}, f32[21,39,672]{2,1,0:T(8,128)}, u32[]{:S(2)}) copy-start(f32[21,39,672]{2,1,0:T(8,128)} %x_ref.1) | copy-start | bytes 6604420
  5.2 2.1 %collective-permute-start = (f32[1056,128]{1,0:T(8,128)S(1)}, f32[1056,128]{1,0:T(8,128)S(1)}, u32[]{:S(2)}, u32[]{:S(2)}) collective-permute-start(f32[1056,128]{1,0:T(8,128)S(1)} %constant_dynamic-slice_fusion.2), channel_id=1, source_target_pairs={{0,4},{1,5},{2,6},{3,7},{4,0},{5,1},{6,2},{7,3},{8,12},{9,13},{10,... | collective-permute-start | bytes 1622024 | tf_op jit(solution)/shard_map/ppermute | solution.py:118
  7.4 7.4 %collective-permute-start.1 = (f32[528,128]{1,0:T(8,128)S(1)}, f32[528,128]{1,0:T(8,128)S(1)}, u32[]{:S(2)}, u32[]{:S(2)}) collective-permute-start(f32[528,128]{1,0:T(8,128)S(1)} %constant_dynamic-slice_fusion.1), channel_id=1, source_target_pairs={{0,8},{1,9},{2,10},{3,11},{4,20},{5,21},{6,22},{7,23},{8,0},{9,1},... | collective-permute-start | bytes 811016 | tf_op jit(solution)/shard_map/ppermute | solution.py:118
  14.8 5.1 %collective-permute-start.2 = (f32[264,128]{1,0:T(8,128)S(1)}, f32[264,128]{1,0:T(8,128)S(1)}, u32[]{:S(2)}, u32[]{:S(2)}) collective-permute-start(f32[264,128]{1,0:T(8,128)S(1)} %constant_dynamic-slice_fusion), channel_id=1, source_target_pairs={{0,16},{1,17},{2,18},{3,19},{4,12},{5,13},{6,14},{7,15},{8,24},{9,... | collective-permute-start | bytes 405512 | tf_op jit(solution)/shard_map/ppermute | solution.py:118
  19.9 5.5 %collective-permute-start.3 = (f32[264,128]{1,0:T(8,128)S(1)}, f32[264,128]{1,0:T(8,128)S(1)}, u32[]{:S(2)}, u32[]{:S(2)}) collective-permute-start(f32[264,128]{1,0:T(8,128)S(1)} %dynamic-slice_add_fusion.2), channel_id=1, source_target_pairs={{0,1},{1,0},{2,3},{3,2},{4,6},{5,7},{6,4},{7,5},{8,9},{9,8},{10,11... | collective-permute-start | bytes 405512 | tf_op jit(solution)/shard_map/ppermute | solution.py:118
  25.5 6.0 %collective-permute-start.4 = (f32[264,128]{1,0:T(8,128)S(1)}, f32[264,128]{1,0:T(8,128)S(1)}, u32[]{:S(2)}, u32[]{:S(2)}) collective-permute-start(f32[264,128]{1,0:T(8,128)S(1)} %add.38), channel_id=1, source_target_pairs={{0,2},{1,3},{2,0},{3,1},{4,5},{5,4},{6,7},{7,6},{8,10},{9,11},{10,... | collective-permute-start | bytes 405512 | tf_op jit(solution)/shard_map/ppermute | solution.py:118
  31.5 7.8 %collective-permute-start.5 = (f32[264,128]{1,0:T(8,128)S(1)}, f32[264,128]{1,0:T(8,128)S(1)}, u32[]{:S(2)}, u32[]{:S(2)}) collective-permute-start(f32[264,128]{1,0:T(8,128)S(1)} %add.39), channel_id=1, source_target_pairs={{0,16},{1,17},{2,18},{3,19},{4,12},{5,13},{6,14},{7,15},{8,24},{9,... | collective-permute-start | bytes 405512 | tf_op jit(solution)/shard_map/ppermute | solution.py:118
  39.3 7.5 %copy-start.1 = (f32[21,39,672]{2,1,0:T(8,128)S(1)}, f32[21,39,672]{2,1,0:T(8,128)}, u32[]{:S(2)}) copy-start(f32[21,39,672]{2,1,0:T(8,128)} %x_ref.1) | copy-start | bytes 6604420
  39.4 6.5 %collective-permute-start.6 = (f32[528,128]{1,0:T(8,128)S(1)}, f32[528,128]{1,0:T(8,128)S(1)}, u32[]{:S(2)}, u32[]{:S(2)}) collective-permute-start(f32[528,128]{1,0:T(8,128)S(1)} %pad_maximum_fusion.2), channel_id=1, source_target_pairs={{0,8},{1,9},{2,10},{3,11},{4,20},{5,21},{6,22},{7,23},{8,0},{9,1},... | collective-permute-start | bytes 811016 | tf_op jit(solution)/shard_map/ppermute | solution.py:118
  46.8 5.4 %collective-permute-start.7 = (f32[1056,128]{1,0:T(8,128)}, f32[1056,128]{1,0:T(8,128)}, u32[]{:S(2)}, u32[]{:S(2)}) collective-permute-start(f32[1056,128]{1,0:T(8,128)} %pad_maximum_fusion.1), channel_id=1, source_target_pairs={{0,4},{1,5},{2,6},{3,7},{4,0},{5,1},{6,2},{7,3},{8,12},{9,13},{10,... | collective-permute-start | bytes 1622024 | tf_op jit(solution)/shard_map/ppermute | solution.py:118
  53.3 1.0 copy-start.2
  53.3 1.0 copy-start.3
where the time goes:
time: 111 us; the launch traced here: 110 us
  Pallas kernels  45.8 us (41%)
  waiting for transfers between devices  24.5 us (22%)
  starting transfers between devices  15.9 us (14%)
  blocking collectives  13.2 us (12%)
  local copies, waits for them, and re-layouts  7.75 us (7%)
  other arithmetic  2.59 us (2%)
    pallas_call x1, Pallas kernels, subspace_step(): pl.pallas_call(subspace_kernel, in_specs=[pl.BlockSpec(memory_space=pltpu...  41.4 us
    ppermute x8, waiting for transfers between devices, swap(): return lax.ppermute(data, ('gx', 'gy'), pairs)  24.5 us
    ppermute x8, starting transfers between devices, swap(): return lax.ppermute(data, ('gx', 'gy'), pairs)  15.9 us
    all_to_all x1, blocking collectives, shards(): core = lax.all_to_all(core, 'gx', split_axis=0, concat_axis=0, tiled=True)  13.2 us
    reshape x2, local copies, waits for them, and re-layouts, shards(): x_t = jnp.transpose(species_field, (2, 1, 0)).reshape(order, width)  4.19 us
    pallas_call x1, Pallas kernels, gram_blocks(): pl.pallas_call(gram_kernel, out_shape=jax.ShapeDtypeStruct((packed, LANES...  2.77 us
    unnamed x8, local copies, waits for them, and re-layouts  2.62 us
  transfers between devices with their start and end apart: 8, of which 7 were waited for; matrix products, arithmetic and copies ran while one was open for 5% of the time, Pallas kernels for 0%

commit v1 on v0

v1 whole, which is shorter than its diff:
```python
import functools

import jax
import jax.numpy as jnp
from jax import lax
from jax.experimental import pallas as pl
from jax.experimental.pallas import tpu as pltpu
from jax.sharding import PartitionSpec as P

ITERS = 3
LANES = 128
PANEL = 16
F32 = jnp.float32
BF16 = jnp.bfloat16


def split(value):
    high = value.astype(BF16)
    return high, (value - high.astype(F32)).astype(BF16)


def dot(left, right, left_dim=1, right_dim=0):
    return lax.dot_general(
        left, right, (((left_dim,), (right_dim,)), ((), ())), preferred_element_type=F32
    )


def packed_blocks(order):
    full, rest = divmod(order, LANES)
    blocks, row = {}, 0
    for i in range(full):
        for j in range(i, full):
            blocks[i, j] = row
            row += LANES
    if rest:
        for j in range(full + 1):
            blocks[full, j] = row
            row += rest
    return blocks, row


def pieces_of(first, count, piece):
    done = 0
    while done < count:
        index, at = divmod(first + done, piece)
        step = min(count - done, piece - at)
        yield index, at, done, step
        done += step


def piece_rows(order, parts):
    _, packed = packed_blocks(order)
    return -(-packed // (8 * parts)) * 8


def gram_kernel(me_ref, x_ref, out_ref, flat, high, low):
    slabs, rows, order = x_ref.shape
    parts, piece, _ = out_ref.shape
    pitch = -(-rows // 8) * 8
    for b in range(slabs):
        flat[pl.ds(b * pitch, rows), :] = x_ref[b]
        if pitch > rows:
            flat[pl.ds(b * pitch + rows, pitch - rows), :] = jnp.zeros((pitch - rows, order), F32)
    spare = flat.shape[0] - slabs * pitch
    if spare:
        flat[pl.ds(slabs * pitch, spare), :] = jnp.zeros((spare, order), F32)
    h, l = split(flat[...])
    high[...] = h
    low[...] = l
    full, rest = divmod(order, LANES)
    blocks, packed = packed_blocks(order)
    me = me_ref[0]

    def put(first, value):
        for index, at, begin, count in pieces_of(first, value.shape[0], piece):
            away = me ^ index
            slot = (away & 1) * (parts // 2) + (away >> 1)
            out_ref[slot, pl.ds(at, count), :] = value[begin : begin + count, :]

    for i in range(full):
        rows_i = slice(i * LANES, (i + 1) * LANES)
        cols = slice(i * LANES, full * LANES)
        product = (
            dot(high[:, rows_i], high[:, cols], 0, 0)
            + dot(high[:, rows_i], low[:, cols], 0, 0)
            + dot(low[:, rows_i], high[:, cols], 0, 0)
        )
        for j in range(i, full):
            put(blocks[i, j], product[:, (j - i) * LANES : (j - i + 1) * LANES])
    if rest:
        rows_i = slice(full * LANES, order)
        product = (
            dot(high[:, rows_i], high[...], 0, 0)
            + dot(high[:, rows_i], low[...], 0, 0)
            + dot(low[:, rows_i], high[...], 0, 0)
        )
        for j in range(full):
            put(blocks[full, j], product[:, j * LANES : (j + 1) * LANES])
        corner = product[:, full * LANES :]
        put(blocks[full, full], jnp.concatenate([corner, jnp.zeros((rest, LANES - rest), F32)], axis=1))
    if parts * piece > packed:
        put(packed, jnp.zeros((parts * piece - packed, LANES), F32))


def gram_pieces(me, x, parts):
    slabs, rows, order = x.shape
    depth = -(-slabs * (-(-rows // 8) * 8) // 16) * 16
    vmem = pl.BlockSpec(memory_space=pltpu.VMEM)
    return pl.pallas_call(
        gram_kernel,
        in_specs=[pl.BlockSpec(memory_space=pltpu.SMEM), vmem],
        out_specs=vmem,
        out_shape=jax.ShapeDtypeStruct((parts, piece_rows(order, parts), LANES), F32),
        scratch_shapes=[
            pltpu.VMEM((depth, order), F32),
            pltpu.VMEM((depth, order), BF16),
            pltpu.VMEM((depth, order), BF16),
        ],
        compiler_params=pltpu.CompilerParams(vmem_limit_bytes=32 << 20),
        name="gram",
    )(me, x)


def swap(value, sizes, flip_x, flip_y=(0, 0)):
    count_x, count_y = sizes
    pairs = []
    for i in range(count_x):
        for j in range(count_y):
            pairs.append((i * count_y + j, (i ^ flip_x[i & 1]) * count_y + (j ^ flip_y[i & 1])))
    return lax.ppermute(value, ("gx", "gy"), pairs)


def wide(block, column):
    return jnp.broadcast_to(block[:, column : column + 1], block.shape)


def total(terms):
    while len(terms) > 1:
        last = [terms[-1]] if len(terms) % 2 else []
        terms = [a + b for a, b in zip(terms[::2], terms[1::2])] + last
    return terms[0]


def inverse_factor(work, out):
    size = work.shape[0]
    lane = lax.broadcasted_iota(jnp.int32, (PANEL, size), 1)
    sub = lax.broadcasted_iota(jnp.int32, (PANEL, size), 0)
    lane8 = lax.broadcasted_iota(jnp.int32, (8, size), 1)
    for p in range(0, size, PANEL):
        rows = work[p : p + PANEL, :]
        cols = [wide(rows, p + k) for k in range(PANEL)]
        inside = (lane >= p) & (lane < p + PANEL)
        fwd = jnp.where(inside, jnp.where(lane == sub + p, 1.0, 0.0), rows)
        full = fwd
        inverse = jnp.zeros((PANEL, size), F32)
        for j in range(PANEL):
            pivot = 1.0 / cols[j][j : j + 1, :]
            inverse = jnp.where(sub == j, pivot, inverse)
            factor = cols[j] * pivot
            below = jnp.where(sub > j, factor, 0.0)
            other = jnp.where(sub == j, 0.0, factor)
            fwd = fwd - below * fwd[j : j + 1, :]
            full = full - other * full[j : j + 1, :]
            for k in range(j + 1, PANEL):
                cols[k] = cols[k] - other * cols[k][j : j + 1, :]
        out[p : p + PANEL, :] = jnp.where(lane <= sub + p, fwd * lax.sqrt(inverse), 0.0)
        full = full * inverse
        inside = (lane8 >= p) & (lane8 < p + PANEL)
        for b in range(p + PANEL, size, 8):
            block = work[b : b + 8, :]
            change = total([wide(block, p + k) * full[k : k + 1, :] for k in range(PANEL)])
            work[b : b + 8, :] = jnp.where(inside, 0.0, block) - change


def orthonormal(columns, work, inverse):
    size = columns.shape[1]
    i = lax.broadcasted_iota(jnp.int32, (size, size), 0)
    j = lax.broadcasted_iota(jnp.int32, (size, size), 1)
    both = jnp.concatenate(split(columns), axis=1)
    four = dot(both, both, 0, 0)
    cross_gram = four[:size, :size] + four[size:, size:] + (four[:size, size:] + four[size:, :size])
    diagonal = jnp.where(i == j, cross_gram, 0.0)
    scale_row = lax.rsqrt(jnp.sum(diagonal, axis=0, keepdims=True))
    scale_col = lax.rsqrt(jnp.sum(diagonal, axis=1, keepdims=True))
    work[...] = cross_gram * scale_row * scale_col
    inverse_factor(work, inverse)
    right = jnp.concatenate(split(inverse[...] * scale_row), axis=0)
    product = dot(both, jnp.concatenate([right, right], axis=1), 1, 1)
    return product[:, :size] + product[:, size:]


def subspace_kernel(
    me_ref, ranks_ref, own_ref, sibling_ref, start_ref, xh_ref, xl_ref,
    core_ref, energy_ref, packed, gram_high, gram_low, basis, work, inverse,
):
    order, size = start_ref.shape
    blocks, _ = packed_blocks(order)
    full, rest = divmod(order, LANES)
    parts, piece, _ = packed.shape
    me = me_ref[0]
    for away in range(parts):
        source = sibling_ref if away & 1 else own_ref
        packed[me ^ away] = source[away >> 1]

    trace = jnp.zeros((1, 1), F32)
    for (i, j), first in blocks.items():
        height = LANES if i < full else rest
        width = LANES if j < full else rest
        parted = [packed[index, at : at + count, :] for index, at, _, count in pieces_of(first, height, piece)]
        block = (jnp.concatenate(parted, axis=0) if len(parted) > 1 else parted[0])[:, :width]
        if i == j:
            a = lax.broadcasted_iota(jnp.int32, (height, width), 0)
            b = lax.broadcasted_iota(jnp.int32, (height, width), 1)
            trace = trace + jnp.sum(jnp.where(a == b, block, 0.0), keepdims=True)
        h, l = split(block)
        gram_high[i * LANES : i * LANES + height, j * LANES : j * LANES + width] = h
        gram_low[i * LANES : i * LANES + height, j * LANES : j * LANES + width] = l
        if i != j:
            h, l = split(block.T)
            gram_high[j * LANES : j * LANES + width, i * LANES : i * LANES + height] = h
            gram_low[j * LANES : j * LANES + width, i * LANES : i * LANES + height] = l

    def images(subspace):
        h, l = split(subspace)
        both = dot(gram_high[...], jnp.concatenate([h, l], axis=1))
        return both[:, :size] + both[:, size:] + dot(gram_low[...], h)

    basis[...] = start_ref[...]

    def step(_, carry):
        basis[...] = orthonormal(images(basis[...]), work, inverse)
        return carry

    lax.fori_loop(0, ITERS, step, 0)
    lane = lax.broadcasted_iota(jnp.int32, (1, size), 1)
    masked = basis[...] * jnp.where(lane < ranks_ref[0], 1.0, 0.0)
    h, l = split(masked)
    core = dot(h, xh_ref[...], 0, 0) + dot(h, xl_ref[...], 0, 0) + dot(l, xh_ref[...], 0, 0)
    kept = core_ref.shape[1]
    for p in range(parts):
        away = me ^ p
        core_ref[(away & 1) * (parts // 2) + (away >> 1)] = core[p * kept : (p + 1) * kept, :]
    caught = jnp.sum(masked * images(masked), axis=0, keepdims=True)
    energy_ref[...] = caught / (trace / order)


def subspace_step(me, ranks, own, sibling, start, x_high, x_low):
    order, size = start.shape
    parts, piece = 2 * own.shape[0], own.shape[1]
    vmem = pl.BlockSpec(memory_space=pltpu.VMEM)
    smem = pl.BlockSpec(memory_space=pltpu.SMEM)
    return pl.pallas_call(
        subspace_kernel,
        in_specs=[smem, smem] + [vmem] * 5,
        out_specs=[vmem, vmem],
        out_shape=(
            jax.ShapeDtypeStruct((parts, size // parts, x_high.shape[1]), F32),
            jax.ShapeDtypeStruct((1, size), F32),
        ),
        scratch_shapes=[
            pltpu.VMEM((parts, piece, LANES), F32),
            pltpu.VMEM((order, order), BF16),
            pltpu.VMEM((order, order), BF16),
            pltpu.VMEM((order, size), F32),
            pltpu.VMEM((size, size), F32),
            pltpu.VMEM((size, size), F32),
        ],
        compiler_params=pltpu.CompilerParams(vmem_limit_bytes=32 << 20),
        name="subspace",
    )(me, ranks, own, sibling, start, x_high, x_low)


def arrange_kernel(slabs, me_ref, *refs):
    *block_refs, out_ref, held = refs
    me = me_ref[0]
    for step, ref in enumerate(block_refs):
        for c in range(2):
            held[me ^ (2 * step + c)] = ref[c]
    for c in range(out_ref.shape[0]):
        out_ref[c] = jnp.concatenate(
            [held[s, :, c * slabs : (c + 1) * slabs] for s in range(held.shape[0])], axis=1
        )


def arrange(me, blocks, slabs, rows):
    _, kept, width = blocks[0].shape
    parts = 2 * len(blocks)
    vmem = pl.BlockSpec(memory_space=pltpu.VMEM)
    return pl.pallas_call(
        functools.partial(arrange_kernel, slabs),
        in_specs=[pl.BlockSpec(memory_space=pltpu.SMEM)] + [vmem] * len(blocks),
        out_specs=vmem,
        out_shape=jax.ShapeDtypeStruct((rows, kept, parts * slabs), F32),
        scratch_shapes=[pltpu.VMEM((parts, kept, width), F32)],
        compiler_params=pltpu.CompilerParams(vmem_limit_bytes=32 << 20),
        name="arrange",
    )(me, *blocks)


def shards(sizes, species_field, start_block, trunc_ranks):
    slabs, rows, order = species_field.shape
    count_x, count_y = sizes
    half = count_x // 2
    me = lax.axis_index("gx").astype(jnp.int32)[None]
    sibling = (1, 1)

    pieces = gram_pieces(me, species_field, count_x)
    arrived = swap(pieces[half:], sizes, sibling)
    flat = jnp.transpose(species_field, (1, 0, 2)).reshape(slabs * rows, order)
    partial = [pieces[t] + arrived[t] for t in range(half)]
    arrived = [swap(partial[t], sizes, (2 * t, 2 * t)) for t in range(1, half)]
    arrived, flat = lax.optimization_barrier((arrived, flat))
    value = total([partial[0]] + arrived)
    width = slabs * rows
    field = jnp.pad(flat.T, ((0, 0), (0, -width % LANES)))
    rounded = lax.reduce_precision(field, 8, 7)
    x_high = rounded.astype(BF16)
    x_low = (field - rounded).astype(BF16)
    bits = [1 << b for b in range(count_y.bit_length() - 1)]
    for step, flip in enumerate(zip(bits, reversed(bits))):
        other = swap(value, sizes, (0, 0), flip)
        if step == 0:
            other, x_high, x_low = lax.optimization_barrier((other, x_high, x_low))
        value = value + other
    own = jnp.stack([value] + [swap(value, sizes, (2 * t, 2 * t)) for t in range(1, half)])
    core, energies = subspace_step(
        me, trunc_ranks, own, swap(own, sizes, sibling), start_block, x_high, x_low
    )

    arrived = swap(core[half:], sizes, sibling)
    sends = [jnp.stack([core[t], arrived[t]]) for t in range(half)]
    blocks = [sends[0]] + [swap(sends[t], sizes, (2 * t, 2 * t)) for t in range(1, half)]
    core = arrange(me, blocks, slabs, rows)
    return (jnp.transpose(core, (1, 0, 2)), energies[0])


def solution(mesh):
    sizes = (mesh.shape["gx"], mesh.shape["gy"])
    in_specs = (P("gx", "gy", None), P(), P())
    out_specs = (P("gx", "gy", None), P())
    return jax.shard_map(
        functools.partial(shards, sizes), mesh=mesh, in_specs=in_specs, out_specs=out_specs, check_vma=False
    )
```

time: 111 us -> 69.6 us (0.63)
  Pallas kernels: 45.8 us -> 21.5 us
  blocking collectives: 13.2 us -> 0 us
  waiting for transfers between devices: 24.5 us -> 19.9 us
  local copies, waits for them, and re-layouts: 7.75 us -> 10.4 us
  other arithmetic: 2.59 us -> 0.55 us
    pallas_call x3, Pallas kernels: 45.8 us -> 21.5 us  [the longest x1 17 us: subspace_step(): pl.pallas_call(subspace_kernel, in_specs=[smem, smem] + [vmem] * 5, out_s...]
    all_to_all x1 -> x0, blocking collectives: 13.2 us -> none  [shards(): core = lax.all_to_all(core, 'gx', split_axis=0, concat_axis=0, tiled=True)]
    ppermute x8 -> x14, waiting for transfers between devices: 24.5 us -> 19.9 us  [swap(): return lax.ppermute(value, ('gx', 'gy'), pairs)]
    optimization_barrier x0 -> x1, local copies, waits for them, and re-layouts: none -> 2.43 us  [shards(): arrived, flat = lax.optimization_barrier((arrived, flat))]
    transpose x1, local copies, waits for them, and re-layouts: 0.84 us -> 2.39 us  [shards(): flat = jnp.transpose(species_field, (1, 0, 2)).reshape(slabs * rows, order)]
    select_n x3 -> x0, other arithmetic: 1.18 us -> none  [all_sum(): jnp.where(upper, other, value)]
    unnamed x8 -> x6, local copies, waits for them, and re-layouts: 2.62 us -> 1.73 us
    reshape x2 -> x1, local copies, waits for them, and re-layouts: 4.19 us -> 3.74 us  [shards(): flat = jnp.transpose(species_field, (1, 0, 2)).reshape(slabs * rows, order)]
  transfers between devices with their start and end apart: 8 -> 14, of which waited for: 7 -> 11; matrix products, arithmetic and copies ran while one was open for 5% -> 13% of each run, Pallas kernels for 0% -> 0%
where the time goes in v1:
time: 69.6 us; the launch traced here: 69.4 us
  Pallas kernels  21.5 us (31%)
  waiting for transfers between devices  19.9 us (29%)
  starting transfers between devices  16.3 us (23%)
  local copies, waits for them, and re-layouts  10.4 us (15%)
  between operations  0.75 us (1%)
    ppermute x14, waiting for transfers between devices, swap(): return lax.ppermute(value, ('gx', 'gy'), pairs)  19.9 us
    pallas_call x1, Pallas kernels, subspace_step(): pl.pallas_call(subspace_kernel, in_specs=[smem, smem] + [vmem] * 5, out_s...  17 us
    ppermute x14, starting transfers between devices, swap(): return lax.ppermute(value, ('gx', 'gy'), pairs)  16.3 us
    reshape x1, local copies, waits for them, and re-layouts, shards(): flat = jnp.transpose(species_field, (1, 0, 2)).reshape(slabs * rows, order)  3.74 us
    pallas_call x1, Pallas kernels, gram_pieces(): pl.pallas_call(gram_kernel, in_specs=[pl.BlockSpec(memory_space=pltpu.SME...  2.78 us
    optimization_barrier x1, local copies, waits for them, and re-layouts, shards(): arrived, flat = lax.optimization_barrier((arrived, flat))  2.43 us
    transpose x1, local copies, waits for them, and re-layouts, shards(): flat = jnp.transpose(species_field, (1, 0, 2)).reshape(slabs * rows, order)  2.39 us
    unnamed x6, local copies, waits for them, and re-layouts  1.73 us
  transfers between devices with their start and end apart: 14, of which 11 were waited for; matrix products, arithmetic and copies ran while one was open for 13% of the time, Pallas kernels for 0%

profile of v1, /device:TPU:0, one launch (start us, length us, event | category | flops | bytes accessed | tf_op | source)
XLA Modules:
  0.0 69.4 jit_solution(9796401661841051208)
XLA Ops:
  0.6 1.7 %copy-done = f32[21,39,672]{2,1,0:T(8,128)S(1)} copy-done((f32[21,39,672]{2,1,0:T(8,128)S(1)}, f32[21,39,672]{2,1,0:T(8,128)}, u32[]{:S(2)}) %copy-start) | copy-done | bytes 2201496
  2.4 2.8 %gram.1 = f32[8,264,128]{2,1,0:T(8,128)S(1)} custom-call(s32[1]{0:T(128)} %bitcast.me_ref, f32[21,39,672]{2,1,0:T(8,128)S(1)} %copy-done), custom_call_target="tpu_custom_call" | custom-call | tf_op jit(solution)/shard_map/gram/pallas_call | solution.py:109
  5.2 0.5 collective-permute-start
  5.7 1.6 %collective-permute-done = f32[4,264,128]{2,1,0:T(8,128)S(1)} collective-permute-done((f32[4,264,128]{2,1,0:T(8,128)S(1)}, f32[4,264,128]{2,1,0:T(8,128)S(1)}, u32[]{:S(2)}, u32[]{:S(2)}) %collective-permute-start) | collective-permute-done | bytes 540704 | tf_op jit(solution)/shard_map/ppermute | solution.py:130
  7.3 3.9 %collective-permute-start.3 = (f32[264,128]{1,0:T(8,128)S(1)}, f32[264,128]{1,0:T(8,128)S(1)}, u32[]{:S(2)}, u32[]{:S(2)}) collective-permute-start(f32[264,128]{1,0:T(8,128)S(1)} %get-tuple-element.22), channel_id=1, source_target_pairs={{0,24},{1,25},{2,26},{3,27},{4,28},{5,29},{6,30},{7,31},{8,16},{9,... | collective-permute-start | bytes 405512 | tf_op jit(solution)/shard_map/ppermute | solution.py:130
  11.2 0.5 collective-permute-start.2
  11.7 0.1 collective-permute-start.1
  11.8 2.4 %copy.6 = f32[39,21,672]{2,1,0:T(8,128)} copy(f32[39,21,672]{2,0,1:T(8,128)S(1)} %bitcast.21) | data formatting | bytes 4402944 | tf_op jit(solution)/shard_map/transpose | solution.py:309
  14.2 3.7 %reshape.11 = f32[819,672]{1,0:T(8,128)} reshape(f32[39,21,672]{2,1,0:T(8,128)} %copy.6) | data formatting | bytes 4402944 | tf_op jit(solution)/shard_map/reshape | solution.py:309
  18.0 0.3 collective-permute-done.1
  18.3 1.8 %collective-permute-start.4 = (f32[264,128]{1,0:T(8,128)S(1)}, f32[264,128]{1,0:T(8,128)S(1)}, u32[]{:S(2)}, u32[]{:S(2)}) collective-permute-start(f32[264,128]{1,0:T(8,128)S(1)} %fusion.6), channel_id=1, source_target_pairs={{0,1},{1,0},{2,3},{3,2},{4,6},{5,7},{6,4},{7,5},{8,9},{9,8},{10,11... | collective-permute-start | bytes 405512 | tf_op jit(solution)/shard_map/ppermute | solution.py:130
  20.1 2.4 %copy.7 = f32[819,672]{0,1:T(8,128)S(1)} copy(f32[819,672]{1,0:T(8,128)} %reshape.11) | data formatting | bytes 4402944 | tf_op jit(solution)/shard_map/optimization_barrier | solution.py:312
  22.5 0.3 fusion
  22.9 1.6 %collective-permute-done.4 = f32[264,128]{1,0:T(8,128)S(1)} collective-permute-done((f32[264,128]{1,0:T(8,128)S(1)}, f32[264,128]{1,0:T(8,128)S(1)}, u32[]{:S(2)}, u32[]{:S(2)}) %collective-permute-start.4) | collective-permute-done | bytes 135200 | tf_op jit(solution)/shard_map/ppermute | solution.py:130
  24.5 2.0 %collective-permute-start.5 = (f32[264,128]{1,0:T(8,128)S(1)}, f32[264,128]{1,0:T(8,128)S(1)}, u32[]{:S(2)}, u32[]{:S(2)}) collective-permute-start(f32[264,128]{1,0:T(8,128)S(1)} %add.52), channel_id=1, source_target_pairs={{0,2},{1,3},{2,0},{3,1},{4,5},{5,4},{6,7},{7,6},{8,10},{9,11},{10,... | collective-permute-start | bytes 405512 | tf_op jit(solution)/shard_map/ppermute | solution.py:130
  26.5 4.0 %collective-permute-done.5 = f32[264,128]{1,0:T(8,128)S(1)} collective-permute-done((f32[264,128]{1,0:T(8,128)S(1)}, f32[264,128]{1,0:T(8,128)S(1)}, u32[]{:S(2)}, u32[]{:S(2)}) %collective-permute-start.5) | collective-permute-done | bytes 135200 | tf_op jit(solution)/shard_map/ppermute | solution.py:130
  30.6 1.8 %collective-permute-start.8 = (f32[264,128]{1,0:T(8,128)S(1)}, f32[264,128]{1,0:T(8,128)S(1)}, u32[]{:S(2)}, u32[]{:S(2)}) collective-permute-start(f32[264,128]{1,0:T(8,128)S(1)} %add.53), channel_id=1, source_target_pairs={{0,24},{1,25},{2,26},{3,27},{4,28},{5,29},{6,30},{7,31},{8,16},{9,... | collective-permute-start | bytes 405512 | tf_op jit(solution)/shard_map/ppermute | solution.py:130
  32.4 1.2 %collective-permute-start.7 = (f32[264,128]{1,0:T(8,128)S(1)}, f32[264,128]{1,0:T(8,128)S(1)}, u32[]{:S(2)}, u32[]{:S(2)}) collective-permute-start(f32[264,128]{1,0:T(8,128)S(1)} %add.53), channel_id=1, source_target_pairs={{0,16},{1,17},{2,18},{3,19},{4,20},{5,21},{6,22},{7,23},{8,24},{9,... | collective-permute-start | bytes 405512 | tf_op jit(solution)/shard_map/ppermute | solution.py:130
  33.6 0.5 collective-permute-start.6
  34.1 2.9 %collective-permute-done.8 = f32[264,128]{1,0:T(8,128)S(1)} collective-permute-done((f32[264,128]{1,0:T(8,128)S(1)}, f32[264,128]{1,0:T(8,128)S(1)}, u32[]{:S(2)}, u32[]{:S(2)}) %collective-permute-start.8) | collective-permute-done | bytes 135200 | tf_op jit(solution)/shard_map/ppermute | solution.py:130
  37.0 1.3 %collective-permute-done.7 = f32[264,128]{1,0:T(8,128)S(1)} collective-permute-done((f32[264,128]{1,0:T(8,128)S(1)}, f32[264,128]{1,0:T(8,128)S(1)}, u32[]{:S(2)}, u32[]{:S(2)}) %collective-permute-start.7) | collective-permute-done | bytes 135200 | tf_op jit(solution)/shard_map/ppermute | solution.py:130
  38.3 0.3 collective-permute-done.6
  38.7 1.9 %collective-permute-done.9.sibling_ref = f32[4,264,128]{2,1,0:T(8,128)S(1)} collective-permute-done((f32[4,264,128]{2,1,0:T(8,128)S(1)}, f32[4,264,128]{2,1,0:T(8,128)S(1)}, u32[]{:S(2)}, u32[]{:S(2)}) %collective-permute-start.9) | collective-permute-done | bytes 540704 | tf_op jit(solution)/shard_map/ppermute | solution.py:130
  40.7 17.0 %subspace.1 = (f32[8,16,896]{2,1,0:T(8,128)S(1)}, f32[1,128]{1,0:T(1,128)}) custom-call(s32[1]{0:T(128)} %bitcast.me_ref, s32[3]{0:T(128)S(1)} %copy-done.2, f32[4,264,128]{2,1,0:T(8,128)S(1)} %pad_maximum_fusion.own_ref, f32[4,264,128]{2,1,0:T(8,128)S(1)} %collective-permute-done.9.sibling_ref, f32[672,128]{1,0:T(8,128)S(1)} %copy-done.1, ...), custom_call_target="tpu_custom_call" | custom-call | tf_op jit(solution)/shard_map/subspace/pallas_call | solution.py:252
  57.7 0.2 collective-permute-start.10
  57.9 1.3 %collective-permute-done.10 = f32[4,16,896]{2,1,0:T(8,128)S(1)} collective-permute-done((f32[4,16,896]{2,1,0:T(8,128)S(1)}, f32[4,16,896]{2,1,0:T(8,128)S(1)}, u32[]{:S(2)}, u32[]{:S(2)}) %collective-permute-start.10) | collective-permute-done | bytes 229408 | tf_op jit(solution)/shard_map/ppermute | solution.py:130
  59.3 0.9 %collective-permute-start.11 = (f32[2,16,896]{2,1,0:T(8,128)S(1)}, f32[2,16,896]{2,1,0:T(8,128)S(1)}, u32[]{:S(2)}, u32[]{:S(2)}) collective-permute-start(f32[2,16,896]{2,1,0:T(8,128)S(1)} %pad_maximum_fusion.2), channel_id=1, source_target_pairs={{0,8},{1,9},{2,10},{3,11},{4,12},{5,13},{6,14},{7,15},{8,0},{9,1},... | collective-permute-start | bytes 344072 | tf_op jit(solution)/shard_map/ppermute | solution.py:130
  60.2 1.2 %collective-permute-start.12 = (f32[2,16,896]{2,1,0:T(8,128)S(1)}, f32[2,16,896]{2,1,0:T(8,128)S(1)}, u32[]{:S(2)}, u32[]{:S(2)}) collective-permute-start(f32[2,16,896]{2,1,0:T(8,128)S(1)} %pad_maximum_fusion.3), channel_id=1, source_target_pairs={{0,16},{1,17},{2,18},{3,19},{4,20},{5,21},{6,22},{7,23},{8,24},{9,... | collective-permute-start | bytes 344072 | tf_op jit(solution)/shard_map/ppermute | solution.py:130
  61.5 1.5 %collective-permute-start.13 = (f32[2,16,896]{2,1,0:T(8,128)S(1)}, f32[2,16,896]{2,1,0:T(8,128)S(1)}, u32[]{:S(2)}, u32[]{:S(2)}) collective-permute-start(f32[2,16,896]{2,1,0:T(8,128)S(1)} %pad_maximum_fusion.4), channel_id=1, source_target_pairs={{0,24},{1,25},{2,26},{3,27},{4,28},{5,29},{6,30},{7,31},{8,16},{9,... | collective-permute-start | bytes 344072 | tf_op jit(solution)/shard_map/ppermute | solution.py:130
  63.0 2.0 %collective-permute-done.11.refs_1_ = f32[2,16,896]{2,1,0:T(8,128)S(1)} collective-permute-done((f32[2,16,896]{2,1,0:T(8,128)S(1)}, f32[2,16,896]{2,1,0:T(8,128)S(1)}, u32[]{:S(2)}, u32[]{:S(2)}) %collective-permute-start.11) | collective-permute-done | bytes 114720 | tf_op jit(solution)/shard_map/ppermute | solution.py:130
  65.0 2.6 %collective-permute-done.12.refs_2_ = f32[2,16,896]{2,1,0:T(8,128)S(1)} collective-permute-done((f32[2,16,896]{2,1,0:T(8,128)S(1)}, f32[2,16,896]{2,1,0:T(8,128)S(1)}, u32[]{:S(2)}, u32[]{:S(2)}) %collective-permute-start.12) | collective-permute-done | bytes 114720 | tf_op jit(solution)/shard_map/ppermute | solution.py:130
  67.7 1.7 %arrange.1 = f32[39,16,168]{2,1,0:T(8,128)} custom-call(s32[1]{0:T(128)} %bitcast.me_ref, f32[2,16,896]{2,1,0:T(8,128)S(1)} %pad_maximum_fusion.1.refs_0_, f32[2,16,896]{2,1,0:T(8,128)S(1)} %collective-permute-done.11.refs_1_, f32[2,16,896]{2,1,0:T(8,128)S(1)} %collective-permute-done.12.refs_2_, f32[2,16,896]{2,1,0:T(8,128)S(1)} %collective-permute-done.13.refs_3_), custom_call_target="tpu_custom_call" | custom-call | tf_op jit(solution)/shard_map/arrange/pallas_call | solution.py:289
  (22 shorter events, 0.4 us)
Async XLA Ops:
  0.6 1.7 %copy-start = (f32[21,39,672]{2,1,0:T(8,128)S(1)}, f32[21,39,672]{2,1,0:T(8,128)}, u32[]{:S(2)}) copy-start(f32[21,39,672]{2,1,0:T(8,128)} %x_ref.1) | copy-start | bytes 6604420
  5.2 2.1 %collective-permute-start = (f32[4,264,128]{2,1,0:T(8,128)S(1)}, f32[4,264,128]{2,1,0:T(8,128)S(1)}, u32[]{:S(2)}, u32[]{:S(2)}) collective-permute-start(f32[4,264,128]{2,1,0:T(8,128)S(1)} %slice.73), channel_id=1, source_target_pairs={{0,4},{1,5},{2,6},{3,7},{4,0},{5,1},{6,2},{7,3},{8,12},{9,13},{10,... | collective-permute-start | bytes 1622024 | tf_op jit(solution)/shard_map/ppermute | solution.py:130
  7.3 10.7 %collective-permute-start.3 = (f32[264,128]{1,0:T(8,128)S(1)}, f32[264,128]{1,0:T(8,128)S(1)}, u32[]{:S(2)}, u32[]{:S(2)}) collective-permute-start(f32[264,128]{1,0:T(8,128)S(1)} %get-tuple-element.22), channel_id=1, source_target_pairs={{0,24},{1,25},{2,26},{3,27},{4,28},{5,29},{6,30},{7,31},{8,16},{9,... | collective-permute-start | bytes 405512 | tf_op jit(solution)/shard_map/ppermute | solution.py:130
  11.2 6.8 %collective-permute-start.2 = (f32[264,128]{1,0:T(8,128)S(1)}, f32[264,128]{1,0:T(8,128)S(1)}, u32[]{:S(2)}, u32[]{:S(2)}) collective-permute-start(f32[264,128]{1,0:T(8,128)S(1)} %get-tuple-element.23), channel_id=1, source_target_pairs={{0,16},{1,17},{2,18},{3,19},{4,20},{5,21},{6,22},{7,23},{8,24},{9,... | collective-permute-start | bytes 405512 | tf_op jit(solution)/shard_map/ppermute | solution.py:130
  11.7 6.6 %collective-permute-start.1 = (f32[264,128]{1,0:T(8,128)S(1)}, f32[264,128]{1,0:T(8,128)S(1)}, u32[]{:S(2)}, u32[]{:S(2)}) collective-permute-start(f32[264,128]{1,0:T(8,128)S(1)} %get-tuple-element.24), channel_id=1, source_target_pairs={{0,8},{1,9},{2,10},{3,11},{4,12},{5,13},{6,14},{7,15},{8,0},{9,1},... | collective-permute-start | bytes 405512 | tf_op jit(solution)/shard_map/ppermute | solution.py:130
  18.3 6.2 %collective-permute-start.4 = (f32[264,128]{1,0:T(8,128)S(1)}, f32[264,128]{1,0:T(8,128)S(1)}, u32[]{:S(2)}, u32[]{:S(2)}) collective-permute-start(f32[264,128]{1,0:T(8,128)S(1)} %fusion.6), channel_id=1, source_target_pairs={{0,1},{1,0},{2,3},{3,2},{4,6},{5,7},{6,4},{7,5},{8,9},{9,8},{10,11... | collective-permute-start | bytes 405512 | tf_op jit(solution)/shard_map/ppermute | solution.py:130
  22.5 18.1 %copy-start.1 = (f32[672,128]{1,0:T(8,128)S(1)}, f32[672,128]{1,0:T(8,128)}, u32[]{:S(2)}) copy-start(f32[672,128]{1,0:T(8,128)} %start_ref.1) | copy-start | bytes 1032196
  22.5 18.1 %copy-start.2 = (s32[3]{0:T(128)S(1)}, s32[3]{0:T(128)}, u32[]{:S(2)}) copy-start(s32[3]{0:T(128)} %ranks_ref.1) | copy-start | bytes 40
  24.5 6.0 %collective-permute-start.5 = (f32[264,128]{1,0:T(8,128)S(1)}, f32[264,128]{1,0:T(8,128)S(1)}, u32[]{:S(2)}, u32[]{:S(2)}) collective-permute-start(f32[264,128]{1,0:T(8,128)S(1)} %add.52), channel_id=1, source_target_pairs={{0,2},{1,3},{2,0},{3,1},{4,5},{5,4},{6,7},{7,6},{8,10},{9,11},{10,... | collective-permute-start | bytes 405512 | tf_op jit(solution)/shard_map/ppermute | solution.py:130
  30.6 6.4 %collective-permute-start.8 = (f32[264,128]{1,0:T(8,128)S(1)}, f32[264,128]{1,0:T(8,128)S(1)}, u32[]{:S(2)}, u32[]{:S(2)}) collective-permute-start(f32[264,128]{1,0:T(8,128)S(1)} %add.53), channel_id=1, source_target_pairs={{0,24},{1,25},{2,26},{3,27},{4,28},{5,29},{6,30},{7,31},{8,16},{9,... | collective-permute-start | bytes 405512 | tf_op jit(solution)/shard_map/ppermute | solution.py:130
  32.4 5.9 %collective-permute-start.7 = (f32[264,128]{1,0:T(8,128)S(1)}, f32[264,128]{1,0:T(8,128)S(1)}, u32[]{:S(2)}, u32[]{:S(2)}) collective-permute-start(f32[264,128]{1,0:T(8,128)S(1)} %add.53), channel_id=1, source_target_pairs={{0,16},{1,17},{2,18},{3,19},{4,20},{5,21},{6,22},{7,23},{8,24},{9,... | collective-permute-start | bytes 405512 | tf_op jit(solution)/shard_map/ppermute | solution.py:130
  33.6 5.0 %collective-permute-start.6 = (f32[264,128]{1,0:T(8,128)S(1)}, f32[264,128]{1,0:T(8,128)S(1)}, u32[]{:S(2)}, u32[]{:S(2)}) collective-permute-start(f32[264,128]{1,0:T(8,128)S(1)} %add.53), channel_id=1, source_target_pairs={{0,8},{1,9},{2,10},{3,11},{4,12},{5,13},{6,14},{7,15},{8,0},{9,1},... | collective-permute-start | bytes 405512 | tf_op jit(solution)/shard_map/ppermute | solution.py:130
  38.7 2.0 %collective-permute-start.9 = (f32[4,264,128]{2,1,0:T(8,128)S(1)}, f32[4,264,128]{2,1,0:T(8,128)S(1)}, u32[]{:S(2)}, u32[]{:S(2)}) collective-permute-start(f32[4,264,128]{2,1,0:T(8,128)S(1)} %pad_maximum_fusion.own_ref), channel_id=1, source_target_pairs={{0,4},{1,5},{2,6},{3,7},{4,0},{5,1},{6,2},{7,3},{8,12},{9,13},{10,... | collective-permute-start | bytes 1622024 | tf_op jit(solution)/shard_map/ppermute | solution.py:130
  57.7 1.6 %collective-permute-start.10 = (f32[4,16,896]{2,1,0:T(8,128)S(1)}, f32[4,16,896]{2,1,0:T(8,128)S(1)}, u32[]{:S(2)}, u32[]{:S(2)}) collective-permute-start(f32[4,16,896]{2,1,0:T(8,128)S(1)} %slice.64), channel_id=1, source_target_pairs={{0,4},{1,5},{2,6},{3,7},{4,0},{5,1},{6,2},{7,3},{8,12},{9,13},{10,... | collective-permute-start | bytes 688136 | tf_op jit(solution)/shard_map/ppermute | solution.py:130
  59.3 5.8 %collective-permute-start.11 = (f32[2,16,896]{2,1,0:T(8,128)S(1)}, f32[2,16,896]{2,1,0:T(8,128)S(1)}, u32[]{:S(2)}, u32[]{:S(2)}) collective-permute-start(f32[2,16,896]{2,1,0:T(8,128)S(1)} %pad_maximum_fusion.2), channel_id=1, source_target_pairs={{0,8},{1,9},{2,10},{3,11},{4,12},{5,13},{6,14},{7,15},{8,0},{9,1},... | collective-permute-start | bytes 344072 | tf_op jit(solution)/shard_map/ppermute | solution.py:130
  60.2 7.4 %collective-permute-start.12 = (f32[2,16,896]{2,1,0:T(8,128)S(1)}, f32[2,16,896]{2,1,0:T(8,128)S(1)}, u32[]{:S(2)}, u32[]{:S(2)}) collective-permute-start(f32[2,16,896]{2,1,0:T(8,128)S(1)} %pad_maximum_fusion.3), channel_id=1, source_target_pairs={{0,16},{1,17},{2,18},{3,19},{4,20},{5,21},{6,22},{7,23},{8,24},{9,... | collective-permute-start | bytes 344072 | tf_op jit(solution)/shard_map/ppermute | solution.py:130
  61.5 6.2 %collective-permute-start.13 = (f32[2,16,896]{2,1,0:T(8,128)S(1)}, f32[2,16,896]{2,1,0:T(8,128)S(1)}, u32[]{:S(2)}, u32[]{:S(2)}) collective-permute-start(f32[2,16,896]{2,1,0:T(8,128)S(1)} %pad_maximum_fusion.4), channel_id=1, source_target_pairs={{0,24},{1,25},{2,26},{3,27},{4,28},{5,29},{6,30},{7,31},{8,16},{9,... | collective-permute-start | bytes 344072 | tf_op jit(solution)/shard_map/ppermute | solution.py:130
